TPU v7x, 32 devices: a whole 2x2x4 slice. The times are simulated.
32 devices in a mesh: grp: 2 (over y), gen: 4 (over z), row: 2 (over x), ch: 2 (over core).
Axes of the slice: x: 2, y: 2, z: 4, core: 2. Of those that a mesh axis runs over, the one named last changes fastest.
Arguments:
- x_center: bfloat16 [24, 24, 112], P(('grp', 'row')), parts along dimension 0, may hold values from -6 to 6
- x_gens: bfloat16 [256, 12, 24, 112], P(('grp', 'gen'), 'row'), parts along dimension 0, may hold values from -0.125 to 0.125
- w_expand: bfloat16 [112, 672], P(None, 'ch'), may hold values from -0.5 to 0.5
- b_expand: float32 [672], P('ch'), may hold values from -3 to 3
- w_depth: float32 [5, 5, 672], P(None, None, 'ch'), may hold values from -1.25 to 1.25
- b_depth: float32 [672], P('ch'), may hold values from -3 to 3
- w_reduce: float32 [672, 28], replicated, may hold values from -0.25 to 0.25
- b_reduce: float32 [28], replicated, may hold values from -6 to 6
- w_excite: float32 [28, 672], P(None, 'ch'), may hold values from -1 to 1
- b_excite: float32 [672], P('ch'), may hold values from -3 to 3
Outputs:
- out_center: float32 [24, 24, 672], P(('grp', 'row'), None, 'ch'), parts along dimension 0
- out_gens: bfloat16 [256, 12, 24, 672], P(('grp', 'gen'), 'row', None, 'ch'), parts along dimension 0
- out_box: float32 [24, 24, 672], P(('grp', 'row'), None, 'ch'), parts along dimension 0
There are 2 independent parts, one for each index of `grp`. A program takes and returns all parts, laid end to end along the dimension named above; an argument that names none is the same for every part. Nothing has to cross between parts.
All inputs are finite; a program needn't handle non-finite values.
Results may differ from a plain program's by a relative error of at most 0.007.
Values may be sent and summed in bfloat16 or wider, within the bound.
A program may use at most 64 MiB of HBM per device.

v0:
```python
import jax
import jax.numpy as jnp
from jax import lax
from jax.sharding import PartitionSpec as P


def padded_2(cells, sides, width):
    for axis, dim in sides:
        count = lax.axis_size(axis)
        ends = count - 1
        head = lax.slice_in_dim(cells, 0, width, axis=dim)
        tail = lax.slice_in_dim(cells, cells.shape[dim] - width, cells.shape[dim], axis=dim)
        cells = jnp.concatenate(
            [
                lax.ppermute(tail, axis, [(i, (i + 1) % count) for i in range(ends)]),
                cells,
                lax.ppermute(head, axis, [((i + 1) % count, i) for i in range(ends)]),
            ],
            axis=dim,
        )
    return cells


def depthwise(padded, w_depth, row_count, col_count):
    accum_sum = jnp.zeros(padded.shape[:-3] + (row_count, col_count, padded.shape[-1]), jnp.float32)
    for tap_row in range(w_depth.shape[0]):
        for tap_col in range(w_depth.shape[1]):
            window = padded[..., tap_row : tap_row + row_count, tap_col : tap_col + col_count, :]
            accum_sum = accum_sum + window.astype(jnp.float32) * w_depth[tap_row, tap_col]
    return accum_sum


def relax_gate(ex_center, gate_radius):
    low_end = ex_center - gate_radius
    high_end = ex_center + gate_radius
    sig_low = jax.nn.sigmoid(low_end)
    sig_high = jax.nn.sigmoid(high_end)
    slope_val = jnp.minimum(sig_low * (1.0 - sig_low), sig_high * (1.0 - sig_high))
    gate_center = slope_val * ex_center + 0.5 * (
        sig_high + sig_low - slope_val * (high_end + low_end)
    )
    spread_term = 0.5 * (sig_high - sig_low - slope_val * (high_end - low_end))
    return (gate_center, slope_val, spread_term)


def on_device(
    x_center, x_gens, w_expand, b_expand, w_depth, b_depth, w_reduce, b_reduce, w_excite, b_excite
):
    precise = lax.Precision.HIGHEST
    row_count = x_center.shape[0]
    col_count = x_center.shape[1]
    margin = w_depth.shape[0] // 2
    height = row_count * lax.axis_size("row")
    own_center = (
        jnp.dot(x_center, w_expand, preferred_element_type=jnp.float32) + b_expand
    ).astype(jnp.bfloat16)
    own_gens = jnp.dot(x_gens, w_expand, preferred_element_type=jnp.float32).astype(jnp.bfloat16)
    padded_center, exp_gens = (
        padded_2(own_center[None], (("row", 1),), margin),
        padded_2(own_gens, (("row", 1),), margin),
    )
    exp_center = padded_center[0]
    dw_center = (
        depthwise(
            jnp.pad(exp_center, ((0, 0), (margin, margin), (0, 0))), w_depth, row_count, col_count
        )
        + b_depth
    )
    dw_gens = depthwise(
        jnp.pad(exp_gens, ((0, 0), (0, 0), (margin, margin), (0, 0))), w_depth, row_count, col_count
    ).astype(jnp.bfloat16)
    local_radius = jnp.sum(jnp.abs(dw_gens).astype(jnp.float32), axis=0)
    feat_radius = lax.psum(local_radius.astype(jnp.bfloat16), "gen").astype(jnp.float32)
    inv_cells = 1.0 / (height * col_count)
    pool_center = jnp.sum(dw_center, axis=(0, 1)) * inv_cells
    pool_gens = jnp.sum(dw_gens.astype(jnp.float32), axis=(1, 2)) * inv_cells
    pool_center, pool_gens = lax.psum((pool_center, pool_gens), "row")
    pool_center, pool_gens = (
        lax.all_gather(pool_center, "ch", axis=0, tiled=True),
        lax.all_gather(pool_gens, "ch", axis=1, tiled=True),
    )
    sq_center = jnp.dot(pool_center, w_reduce, precision=precise) + b_reduce
    sq_gens = jnp.dot(pool_gens, w_reduce, precision=precise)
    ex_center = jnp.dot(sq_center, w_excite, precision=precise) + b_excite
    ex_gens = jnp.dot(sq_gens, w_excite, precision=precise)
    local_gate = jnp.sum(jnp.abs(ex_gens), axis=0)
    gate_radius = lax.psum(local_gate, "gen")
    gate_center, slope_val, spread_term = relax_gate(ex_center, gate_radius)
    gate_gens = slope_val * ex_gens
    gate_total = slope_val * gate_radius + spread_term
    out_center = dw_center * gate_center
    out_gens = (
        dw_center[None] * gate_gens[:, None, None, :] + gate_center * dw_gens.astype(jnp.float32)
    ).astype(jnp.bfloat16)
    out_box = jnp.abs(dw_center) * spread_term + feat_radius * gate_total
    return (out_center, out_gens, out_box)


def solution(mesh):
    in_specs = (
        P(("grp", "row"), None, None),
        P(("grp", "gen"), "row", None, None),
        P(None, "ch"),
        P("ch"),
        P(None, None, "ch"),
        P("ch"),
        P(),
        P(),
        P(None, "ch"),
        P("ch"),
    )
    out_specs = (
        P(("grp", "row"), None, "ch"),
        P(("grp", "gen"), "row", None, "ch"),
        P(("grp", "row"), None, "ch"),
    )
    return jax.shard_map(
        on_device, mesh=mesh, in_specs=in_specs, out_specs=out_specs, check_vma=False
    )
```

profile of v0, /device:TPU:0, one launch (start us, length us, event | category | flops | bytes accessed | tf_op | source)
XLA Modules:
  0.0 158.3 jit_solution(7868067441693738180)
XLA Ops:
  7.3 1.3 copy-done
  8.5 2.3 %convolution_convert_fusion = bf16[32,6,24,336]{3,2,1,0:T(8,128)(2,1)S(1)} fusion(bf16[32,6,24,112]{3,2,1,0:T(8,128)(2,1)S(1)} %copy-done, bf16[112,336]{1,0:T(8,128)(2,1)} %param.12), kind=kOutput, calls=%fused_computation.22 | convolution fusion | flops 348364800 | bytes 4204032 | tf_op jit(solution)/shard_map/dot_general | solution.py:57
  10.8 1.8 %copy-done.1 = bf16[32,6,24,336]{3,2,1,0:T(8,128)(2,1)} copy-done((bf16[32,6,24,336]{3,2,1,0:T(8,128)(2,1)}, bf16[32,6,24,336]{3,2,1,0:T(8,128)(2,1)S(1)}, u32[]{:S(2)}) %copy-start.1) | copy-done | bytes 3096600
  12.6 1.6 %fusion.48 = (bf16[32,2,24,336]{3,2,1,0:T(8,128)(2,1)}, bf16[32,2,24,336]{3,2,1,0:T(8,128)(2,1)}) fusion(bf16[32,6,24,336]{3,2,1,0:T(8,128)(2,1)S(1)} %convolution_convert_fusion), kind=kLoop, calls=%fused_computation.132 | loop fusion | bytes 4128768 | tf_op jit(solution)/shard_map/slice | solution.py:12
  14.3 4.9 %collective-permute-start.2 = (bf16[32,2,24,336]{3,2,1,0:T(8,128)(2,1)}, bf16[32,2,24,336]{3,2,1,0:T(8,128)(2,1)S(1)}, u32[]{:S(2)}, u32[]{:S(2)}) collective-permute-start(bf16[32,2,24,336]{3,2,1,0:T(8,128)(2,1)} %get-tuple-element.36), channel_id=1, source_target_pairs={{0,2},{1,3},{4,6},{5,7},{8,10},{9,11},{12,14},{13,15},{16,18},{17,... | collective-permute-start | bytes 3096584 | tf_op jit(solution)/shard_map/ppermute | solution.py:15
  19.2 1.3 collective-permute-start.3
  20.7 5.6 %collective-permute-start = (bf16[1,2,24,336]{3,2,1,0:T(8,128)(2,1)S(1)}, bf16[1,2,24,336]{3,2,1,0:T(8,128)(2,1)S(1)}, u32[]{:S(2)}, u32[]{:S(2)}) collective-permute-start(bf16[1,2,24,336]{3,2,1,0:T(8,128)(2,1)S(1)} %get-tuple-element.40), channel_id=1, source_target_pairs={{0,2},{1,3},{4,6},{5,7},{8,10},{9,11},{12,14},{13,15},{16,18},{17,... | collective-permute-start | bytes 96776 | tf_op jit(solution)/shard_map/ppermute | solution.py:15
  26.3 1.3 collective-permute-start.1
  29.2 16.1 %collective-permute-done = bf16[1,2,24,336]{3,2,1,0:T(8,128)(2,1)S(1)} collective-permute-done((bf16[1,2,24,336]{3,2,1,0:T(8,128)(2,1)S(1)}, bf16[1,2,24,336]{3,2,1,0:T(8,128)(2,1)S(1)}, u32[]{:S(2)}, u32[]{:S(2)}) %collective-permute-start) | collective-permute-done | bytes 32288 | tf_op jit(solution)/shard_map/ppermute | solution.py:15
  45.3 4.2 %collective-permute-done.1 = bf16[1,2,24,336]{3,2,1,0:T(8,128)(2,1)S(1)} collective-permute-done((bf16[1,2,24,336]{3,2,1,0:T(8,128)(2,1)S(1)}, bf16[1,2,24,336]{3,2,1,0:T(8,128)(2,1)S(1)}, u32[]{:S(2)}, u32[]{:S(2)}) %collective-permute-start.1) | collective-permute-done | bytes 32288 | tf_op jit(solution)/shard_map/ppermute | solution.py:17
  49.6 1.3 fusion.46
  51.7 1.0 copy-done.4
  52.7 5.7 %fusion.5 = bf16[32,10,28,336]{3,2,1,0:T(8,128)(2,1)S(1)} fusion(bf16[32,2,24,336]{3,2,1,0:T(8,128)(2,1)} %collective-permute-done.3, bf16[32,6,24,336]{3,2,1,0:T(8,128)(2,1)} %copy-done.1, bf16[32,2,24,336]{3,2,1,0:T(8,128)(2,1)} %copy-done.4), kind=kLoop, calls=%fused_computation.9 | loop fusion | flops 36126720 | bytes 11182080 | tf_op jit(solution)/shard_map/concatenate | solution.py:13
  58.5 27.4 %abs_reduce_fusion = (bf16[6,24,336]{2,1,0:T(8,128)(2,1)}, bf16[32,6,24,336]{3,2,1,0:T(8,128)(2,1)S(1)}) fusion(f32[336]{0:T(512)} %copy-done.26, bf16[32,10,28,336]{3,2,1,0:T(8,128)(2,1)S(1)} %fusion.5, f32[336]{0:T(512)} %copy-done.27, f32[336]{0:T(512)S(1)} %get-tuple-element.4, bf16[32,2,24,336]{3,2,1,0:T(8,128)(2,1)} %collective-permute-done.3, ...), kind=kLoop, calls=%fused_computation.21 | loop fusion | flops 125362944 | bytes 70319424 | tf_op jit(solution)/shard_map/reduce_sum | solution.py:72
  85.9 1.8 %copy-done.3 = bf16[32,6,24,336]{3,2,1,0:T(8,128)(2,1)} copy-done((bf16[32,6,24,336]{3,2,1,0:T(8,128)(2,1)}, bf16[32,6,24,336]{3,2,1,0:T(8,128)(2,1)S(1)}, u32[]{:S(2)}) %copy-start.3) | copy-done | bytes 3096600
  88.3 7.8 %all-reduce.3 = (f32[336]{0:T(512)S(1)}, f32[32,336]{1,0:T(8,128)S(1)}) all-reduce(f32[336]{0:T(512)} %broadcast_multiply_fusion.3, f32[32,336]{1,0:T(8,128)S(1)} %broadcast_multiply_fusion.2), channel_id=1, replica_groups=mesh['grp'=2,'gen'=4,'row'=2,'ch'=2] {'row'}, use_global_device_ids=true, to_apply=%region_1.2 | all-reduce | flops 11088 | bytes 88704 | tf_op jit(solution)/shard_map/psum | solution.py:77
  96.1 1.9 %all-gather = f32[2,336,32]{1,2,0:T(8,128)S(1)} all-gather(f32[1,336,32]{1,2,0:T(8,128)S(1)} %bitcast.62), channel_id=1, replica_groups=mesh['grp'=2,'gen'=4,'row'=2,'ch'=2] {'ch'}, dimensions={0}, use_global_device_ids=true | all-gather | bytes 129024 | tf_op jit(solution)/shard_map/all_gather | solution.py:80
  98.4 1.0 abs_reduce_fusion.1
  99.4 12.0 %psum.30 = f32[336]{0:T(512)S(1)} all-reduce(f32[336]{0:T(512)S(1)} %get-tuple-element.45), channel_id=1, replica_groups=mesh['grp'=2,'gen'=4,'row'=2,'ch'=2] {'gen'}, use_global_device_ids=true, to_apply=%region_5.6 | all-reduce | flops 336 | bytes 2688 | tf_op jit(solution)/shard_map/psum | solution.py:87
  111.6 2.4 %all-reduce.2 = f32[672]{0:T(1024)S(1)} all-reduce(f32[672]{0:T(1024)S(1)} %dynamic-update-slice), channel_id=1, replica_groups=mesh['grp'=2,'gen'=4,'row'=2,'ch'=2] {'ch'}, use_global_device_ids=true, to_apply=%add.2 | all-reduce | flops 672 | bytes 5376
  114.9 1.0 convolution_reduce_fusion
  116.7 5.0 %fusion.7 = bf16[32,6,24,336]{3,2,1,0:T(8,128)(2,1)} fusion(bf16[32,6,24,336]{3,2,1,0:T(8,128)(2,1)} %copy-done.3, f32[336]{0:T(512)S(1)} %get-tuple-element.43, f32[32,336]{1,0:T(8,128)S(1)} %broadcast_multiply_fusion.1, f32[6,24,336]{2,1,0:T(8,128)} %get-tuple-element.35), kind=kLoop, calls=%fused_computation.11 | loop fusion | flops 7741440 | bytes 6431040 | tf_op jit(solution)/shard_map/convert_element_type | solution.py:94
  121.7 28.1 %all-reduce.6.cloned.1.call-done = bf16[6,24,336]{2,1,0:T(8,128)(2,1)} async-done(((bf16[6,24,336]{2,1,0:T(8,128)(2,1)}), bf16[6,24,336]{2,1,0:T(8,128)(2,1)}) %all-reduce.6.cloned.1.call-update) | async-done | bytes 96784 | tf_op jit(solution)/shard_map/psum | solution.py:73
  149.7 1.7 %multiply_add_fusion = (f32[6,24,336]{2,1,0:T(8,128)}, f32[6,24,336]{2,1,0:T(8,128)}) fusion(bf16[6,24,336]{2,1,0:T(8,128)(2,1)} %all-reduce.6.cloned.1.call-done, f32[6,24,336]{2,1,0:T(8,128)S(1)} %copy-done.5, f32[336]{0:T(512)S(1)} %get-tuple-element.42, f32[336]{0:T(512)S(1)} %get-tuple-element.30, f32[336]{0:T(512)S(1)} %get-tuple-element.43), kind=kLoop, calls=%fused_computation.77 | loop fusion | flops 290304 | bytes 681408 | tf_op jit(solution)/shard_map/add | solution.py:95
  (81 shorter events, 4.6 us)
Async XLA Ops:
  7.2 42.3 %copy-start.29 = (f32[336]{0:T(512)S(1)}, f32[336]{0:T(512)}, u32[]{:S(2)}) copy-start(f32[336]{0:T(512)} %param.15) | copy-start | bytes 4036
  7.2 142.5 %all-reduce.6.cloned.1.call-start = ((), (), s32[]{:S(2)}) async-start(), calls=%async_computation | async-start | bytes 221184 | tf_op jit(solution)/shard_map/psum | solution.py:73
  14.3 37.2 %collective-permute-start.2 = (bf16[32,2,24,336]{3,2,1,0:T(8,128)(2,1)}, bf16[32,2,24,336]{3,2,1,0:T(8,128)(2,1)S(1)}, u32[]{:S(2)}, u32[]{:S(2)}) collective-permute-start(bf16[32,2,24,336]{3,2,1,0:T(8,128)(2,1)} %get-tuple-element.36), channel_id=1, source_target_pairs={{0,2},{1,3},{4,6},{5,7},{8,10},{9,11},{12,14},{13,15},{16,18},{17,... | collective-permute-start | bytes 3096584 | tf_op jit(solution)/shard_map/ppermute | solution.py:15
  19.2 33.5 %collective-permute-start.3 = (bf16[32,2,24,336]{3,2,1,0:T(8,128)(2,1)}, bf16[32,2,24,336]{3,2,1,0:T(8,128)(2,1)}, u32[]{:S(2)}, u32[]{:S(2)}) collective-permute-start(bf16[32,2,24,336]{3,2,1,0:T(8,128)(2,1)} %get-tuple-element.37), channel_id=1, source_target_pairs={{2,0},{3,1},{6,4},{7,5},{10,8},{11,9},{14,12},{15,13},{18,16},{19,... | collective-permute-start | bytes 3096584 | tf_op jit(solution)/shard_map/ppermute | solution.py:17
  20.7 24.6 %collective-permute-start = (bf16[1,2,24,336]{3,2,1,0:T(8,128)(2,1)S(1)}, bf16[1,2,24,336]{3,2,1,0:T(8,128)(2,1)S(1)}, u32[]{:S(2)}, u32[]{:S(2)}) collective-permute-start(bf16[1,2,24,336]{3,2,1,0:T(8,128)(2,1)S(1)} %get-tuple-element.40), channel_id=1, source_target_pairs={{0,2},{1,3},{4,6},{5,7},{8,10},{9,11},{12,14},{13,15},{16,18},{17,... | collective-permute-start | bytes 96776 | tf_op jit(solution)/shard_map/ppermute | solution.py:15
  26.3 23.2 %collective-permute-start.1 = (bf16[1,2,24,336]{3,2,1,0:T(8,128)(2,1)S(1)}, bf16[1,2,24,336]{3,2,1,0:T(8,128)(2,1)S(1)}, u32[]{:S(2)}, u32[]{:S(2)}) collective-permute-start(bf16[1,2,24,336]{3,2,1,0:T(8,128)(2,1)S(1)} %get-tuple-element.41), channel_id=1, source_target_pairs={{2,0},{3,1},{6,4},{7,5},{10,8},{11,9},{14,12},{15,13},{18,16},{19,... | collective-permute-start | bytes 96776 | tf_op jit(solution)/shard_map/ppermute | solution.py:17
  27.7 23.8 %copy-start.10 = (f32[336]{0:T(512)}, f32[336]{0:T(512)S(1)}, u32[]{:S(2)}) copy-start(f32[336]{0:T(512)S(1)} %get-tuple-element.10) | copy-start | bytes 4036
  27.7 23.8 %copy-start.11 = (f32[336]{0:T(512)}, f32[336]{0:T(512)S(1)}, u32[]{:S(2)}) copy-start(f32[336]{0:T(512)S(1)} %get-tuple-element.11) | copy-start | bytes 4036
  27.7 23.8 %copy-start.12 = (f32[336]{0:T(512)}, f32[336]{0:T(512)S(1)}, u32[]{:S(2)}) copy-start(f32[336]{0:T(512)S(1)} %get-tuple-element.12) | copy-start | bytes 4036
  27.7 23.8 %copy-start.13 = (f32[336]{0:T(512)}, f32[336]{0:T(512)S(1)}, u32[]{:S(2)}) copy-start(f32[336]{0:T(512)S(1)} %get-tuple-element.13) | copy-start | bytes 4036
  27.7 23.8 %copy-start.14 = (f32[336]{0:T(512)}, f32[336]{0:T(512)S(1)}, u32[]{:S(2)}) copy-start(f32[336]{0:T(512)S(1)} %get-tuple-element.14) | copy-start | bytes 4036
  27.7 23.8 %copy-start.15 = (f32[336]{0:T(512)}, f32[336]{0:T(512)S(1)}, u32[]{:S(2)}) copy-start(f32[336]{0:T(512)S(1)} %get-tuple-element.15) | copy-start | bytes 4036
  27.8 23.8 %copy-start.16 = (f32[336]{0:T(512)}, f32[336]{0:T(512)S(1)}, u32[]{:S(2)}) copy-start(f32[336]{0:T(512)S(1)} %get-tuple-element.16) | copy-start | bytes 4036
  27.8 23.8 %copy-start.17 = (f32[336]{0:T(512)}, f32[336]{0:T(512)S(1)}, u32[]{:S(2)}) copy-start(f32[336]{0:T(512)S(1)} %get-tuple-element.17) | copy-start | bytes 4036
  27.8 23.8 %copy-start.18 = (f32[336]{0:T(512)}, f32[336]{0:T(512)S(1)}, u32[]{:S(2)}) copy-start(f32[336]{0:T(512)S(1)} %get-tuple-element.18) | copy-start | bytes 4036
  27.8 23.8 %copy-start.19 = (f32[336]{0:T(512)}, f32[336]{0:T(512)S(1)}, u32[]{:S(2)}) copy-start(f32[336]{0:T(512)S(1)} %get-tuple-element.19) | copy-start | bytes 4036
  27.8 23.8 %copy-start.20 = (f32[336]{0:T(512)}, f32[336]{0:T(512)S(1)}, u32[]{:S(2)}) copy-start(f32[336]{0:T(512)S(1)} %get-tuple-element.20) | copy-start | bytes 4036
  27.8 23.8 %copy-start.21 = (f32[336]{0:T(512)}, f32[336]{0:T(512)S(1)}, u32[]{:S(2)}) copy-start(f32[336]{0:T(512)S(1)} %get-tuple-element.21) | copy-start | bytes 4036
  27.9 23.8 %copy-start.23 = (f32[336]{0:T(512)}, f32[336]{0:T(512)S(1)}, u32[]{:S(2)}) copy-start(f32[336]{0:T(512)S(1)} %get-tuple-element.23) | copy-start | bytes 4036
  27.9 23.8 %copy-start.24 = (f32[336]{0:T(512)}, f32[336]{0:T(512)S(1)}, u32[]{:S(2)}) copy-start(f32[336]{0:T(512)S(1)} %get-tuple-element.24) | copy-start | bytes 4036
  27.9 23.8 %copy-start.25 = (f32[336]{0:T(512)}, f32[336]{0:T(512)S(1)}, u32[]{:S(2)}) copy-start(f32[336]{0:T(512)S(1)} %get-tuple-element.25) | copy-start | bytes 4036
  27.9 23.8 %copy-start.26 = (f32[336]{0:T(512)}, f32[336]{0:T(512)S(1)}, u32[]{:S(2)}) copy-start(f32[336]{0:T(512)S(1)} %get-tuple-element.26) | copy-start | bytes 4036
  58.4 39.7 %copy-start.6 = (f32[672,28]{0,1:T(8,128)S(1)}, f32[672,28]{0,1:T(8,128)}, u32[]{:S(2)}) copy-start(f32[672,28]{0,1:T(8,128)} %param.16) | copy-start | bytes 225796
  85.9 63.9 %copy-start.5 = (f32[6,24,336]{2,1,0:T(8,128)S(1)}, f32[6,24,336]{2,1,0:T(8,128)}, u32[]{:S(2)}) copy-start(f32[6,24,336]{2,1,0:T(8,128)} %get-tuple-element.35) | copy-start | bytes 580612
  (12 other events, 143.3 us)
Sparse Core Ops, SparseCore 0:
  116.8 32.9 all-reduce.5
where the time goes:
time: 159 us; the launch traced here: 158 us
  waiting for transfers between devices  48.4 us (30%)
  other arithmetic  43.2 us (27%)
  blocking collectives  24.1 us (15%)
  between operations  15.2 us (10%)
  starting transfers between devices  13.1 us (8%)
  local copies, waits for them, and re-layouts  8.8 us (6%)
  matrix products  5.47 us (3%)
    psum x1, waiting for transfers between devices, on_device(): lax.psum(local_radius.astype(jnp.bfloat16), 'gen').astype(jnp.float32)  28.1 us
    reduce_sum x1, other arithmetic, on_device(): local_radius = jnp.sum(jnp.abs(dw_gens).astype(jnp.float32), axis=0)  27.4 us
    ppermute x2, waiting for transfers between devices, padded_2(): lax.ppermute(tail, axis, [(i, (i + 1) % count) for i in range(ends)])  16.1 us
    psum x1, blocking collectives, on_device(): gate_radius = lax.psum(local_gate, 'gen')  12 us
    ppermute x2, starting transfers between devices, padded_2(): lax.ppermute(tail, axis, [(i, (i + 1) % count) for i in range(ends)])  10.5 us
    psum x1, blocking collectives, on_device(): pool_center, pool_gens = lax.psum((pool_center, pool_gens), 'row')  7.8 us
    unnamed x67, local copies, waits for them, and re-layouts  6.92 us
    concatenate x1, other arithmetic, padded_2(): jnp.concatenate([lax.ppermute(tail, axis, [(i, (i + 1) % count) for i in...  5.74 us
  transfers between devices with their start and end apart: 5, of which 3 were waited for; matrix products, arithmetic and copies ran while one was open for 5% of the time, Pallas kernels for 0%

commit v1 on v0

--- a/solution.py
+++ b/solution.py
@@ -84,7 +84,11 @@
     ex_center = jnp.dot(sq_center, w_excite, precision=precise) + b_excite
     ex_gens = jnp.dot(sq_gens, w_excite, precision=precise)
     local_gate = jnp.sum(jnp.abs(ex_gens), axis=0)
-    gate_radius = lax.psum(local_gate, "gen")
+    gate_radius = local_gate
+    for hop in (1, 2):
+        gate_radius = gate_radius + lax.ppermute(
+            gate_radius, "gen", [(dev, dev ^ hop) for dev in range(4)]
+        )
     gate_center, slope_val, spread_term = relax_gate(ex_center, gate_radius)
     gate_gens = slope_val * ex_gens
     gate_total = slope_val * gate_radius + spread_term

time: 159 us -> 150 us (0.943)
  blocking collectives: 24.1 us -> 12.1 us
  starting transfers between devices: 13.1 us -> 17.4 us
    psum x1 -> x0, blocking collectives: 12 us -> none  [on_device(): gate_radius = lax.psum(local_gate, 'gen')]
    ppermute x0 -> x2, starting transfers between devices: none -> 4.3 us  [on_device(): lax.ppermute(gate_radius, 'gen', [(dev, dev ^ hop) for dev in range(4)])]
    psum x1, waiting for transfers between devices: 28.1 us -> 26.4 us  [on_device(): lax.psum(local_radius.astype(jnp.bfloat16), 'gen').astype(jnp.float32)]
  transfers between devices with their start and end apart: 5 -> 7, of which waited for: 3 -> 4; matrix products, arithmetic and copies ran while one was open for 5% -> 7% of each run, Pallas kernels for 0% -> 0%
where the time goes in v1:
time: 150 us
  waiting for transfers between devices  47.7 us (32%)
  other arithmetic  43.2 us (29%)
  starting transfers between devices  17.4 us (12%)
  between operations  15.3 us (10%)
  blocking collectives  12.1 us (8%)
  local copies, waits for them, and re-layouts  8.73 us (6%)
  matrix products  5.44 us (4%)
    reduce_sum x1, other arithmetic, on_device(): local_radius = jnp.sum(jnp.abs(dw_gens).astype(jnp.float32), axis=0)  27.4 us
    psum x1, waiting for transfers between devices, on_device(): lax.psum(local_radius.astype(jnp.bfloat16), 'gen').astype(jnp.float32)  26.4 us
    ppermute x2, waiting for transfers between devices, padded_2(): lax.ppermute(tail, axis, [(i, (i + 1) % count) for i in range(ends)])  16.1 us
    ppermute x2, starting transfers between devices, padded_2(): lax.ppermute(tail, axis, [(i, (i + 1) % count) for i in range(ends)])  10.5 us
    psum x1, blocking collectives, on_device(): pool_center, pool_gens = lax.psum((pool_center, pool_gens), 'row')  7.8 us
    unnamed x67, local copies, waits for them, and re-layouts  6.86 us
    concatenate x1, other arithmetic, padded_2(): jnp.concatenate([lax.ppermute(tail, axis, [(i, (i + 1) % count) for i in...  5.74 us
    convert_element_type x1, other arithmetic, on_device(): out_gens = (dw_center[None] * gate_gens[:, None, None, :] + gate_center *...  5 us
  transfers between devices with their start and end apart: 7, of which 4 were waited for; matrix products, arithmetic and copies ran while one was open for 7% of the time, Pallas kernels for 0%

profile of v1, /device:TPU:0, one launch (start us, length us, event | category | flops | bytes accessed | tf_op | source)
XLA Modules:
  0.0 149.8 jit_solution(10648879374320342340)
XLA Ops:
  7.3 1.3 copy-done
  8.5 2.3 %convolution_convert_fusion = bf16[32,6,24,336]{3,2,1,0:T(8,128)(2,1)S(1)} fusion(bf16[32,6,24,112]{3,2,1,0:T(8,128)(2,1)S(1)} %copy-done, bf16[112,336]{1,0:T(8,128)(2,1)} %param.12), kind=kOutput, calls=%fused_computation.22 | convolution fusion | flops 348364800 | bytes 4204032 | tf_op jit(solution)/shard_map/dot_general | solution.py:57
  10.8 1.8 %copy-done.1 = bf16[32,6,24,336]{3,2,1,0:T(8,128)(2,1)} copy-done((bf16[32,6,24,336]{3,2,1,0:T(8,128)(2,1)}, bf16[32,6,24,336]{3,2,1,0:T(8,128)(2,1)S(1)}, u32[]{:S(2)}) %copy-start.1) | copy-done | bytes 3096600
  12.6 1.6 %fusion.48 = (bf16[32,2,24,336]{3,2,1,0:T(8,128)(2,1)}, bf16[32,2,24,336]{3,2,1,0:T(8,128)(2,1)}) fusion(bf16[32,6,24,336]{3,2,1,0:T(8,128)(2,1)S(1)} %convolution_convert_fusion), kind=kLoop, calls=%fused_computation.132 | loop fusion | bytes 4128768 | tf_op jit(solution)/shard_map/slice | solution.py:12
  14.3 4.9 %collective-permute-start.2 = (bf16[32,2,24,336]{3,2,1,0:T(8,128)(2,1)}, bf16[32,2,24,336]{3,2,1,0:T(8,128)(2,1)S(1)}, u32[]{:S(2)}, u32[]{:S(2)}) collective-permute-start(bf16[32,2,24,336]{3,2,1,0:T(8,128)(2,1)} %get-tuple-element.37), channel_id=1, source_target_pairs={{0,2},{1,3},{4,6},{5,7},{8,10},{9,11},{12,14},{13,15},{16,18},{17,... | collective-permute-start | bytes 3096584 | tf_op jit(solution)/shard_map/ppermute | solution.py:15
  19.2 1.3 collective-permute-start.3
  20.7 5.6 %collective-permute-start = (bf16[1,2,24,336]{3,2,1,0:T(8,128)(2,1)S(1)}, bf16[1,2,24,336]{3,2,1,0:T(8,128)(2,1)S(1)}, u32[]{:S(2)}, u32[]{:S(2)}) collective-permute-start(bf16[1,2,24,336]{3,2,1,0:T(8,128)(2,1)S(1)} %get-tuple-element.41), channel_id=1, source_target_pairs={{0,2},{1,3},{4,6},{5,7},{8,10},{9,11},{12,14},{13,15},{16,18},{17,... | collective-permute-start | bytes 96776 | tf_op jit(solution)/shard_map/ppermute | solution.py:15
  26.3 1.3 collective-permute-start.1
  29.2 16.1 %collective-permute-done = bf16[1,2,24,336]{3,2,1,0:T(8,128)(2,1)S(1)} collective-permute-done((bf16[1,2,24,336]{3,2,1,0:T(8,128)(2,1)S(1)}, bf16[1,2,24,336]{3,2,1,0:T(8,128)(2,1)S(1)}, u32[]{:S(2)}, u32[]{:S(2)}) %collective-permute-start) | collective-permute-done | bytes 32288 | tf_op jit(solution)/shard_map/ppermute | solution.py:15
  45.3 4.2 %collective-permute-done.1 = bf16[1,2,24,336]{3,2,1,0:T(8,128)(2,1)S(1)} collective-permute-done((bf16[1,2,24,336]{3,2,1,0:T(8,128)(2,1)S(1)}, bf16[1,2,24,336]{3,2,1,0:T(8,128)(2,1)S(1)}, u32[]{:S(2)}, u32[]{:S(2)}) %collective-permute-start.1) | collective-permute-done | bytes 32288 | tf_op jit(solution)/shard_map/ppermute | solution.py:17
  49.6 1.3 fusion.46
  51.7 1.0 copy-done.4
  52.7 5.7 %fusion.5 = bf16[32,10,28,336]{3,2,1,0:T(8,128)(2,1)S(1)} fusion(bf16[32,2,24,336]{3,2,1,0:T(8,128)(2,1)} %collective-permute-done.3, bf16[32,6,24,336]{3,2,1,0:T(8,128)(2,1)} %copy-done.1, bf16[32,2,24,336]{3,2,1,0:T(8,128)(2,1)} %copy-done.4), kind=kLoop, calls=%fused_computation.9 | loop fusion | flops 36126720 | bytes 11182080 | tf_op jit(solution)/shard_map/concatenate | solution.py:13
  58.5 27.4 %abs_reduce_fusion = (bf16[6,24,336]{2,1,0:T(8,128)(2,1)}, bf16[32,6,24,336]{3,2,1,0:T(8,128)(2,1)S(1)}) fusion(f32[336]{0:T(512)} %copy-done.26, bf16[32,10,28,336]{3,2,1,0:T(8,128)(2,1)S(1)} %fusion.5, f32[336]{0:T(512)} %copy-done.27, f32[336]{0:T(512)S(1)} %get-tuple-element.4, bf16[32,2,24,336]{3,2,1,0:T(8,128)(2,1)} %collective-permute-done.3, ...), kind=kLoop, calls=%fused_computation.21 | loop fusion | flops 125362944 | bytes 70319424 | tf_op jit(solution)/shard_map/reduce_sum | solution.py:72
  85.9 1.8 %copy-done.3 = bf16[32,6,24,336]{3,2,1,0:T(8,128)(2,1)} copy-done((bf16[32,6,24,336]{3,2,1,0:T(8,128)(2,1)}, bf16[32,6,24,336]{3,2,1,0:T(8,128)(2,1)S(1)}, u32[]{:S(2)}) %copy-start.3) | copy-done | bytes 3096600
  88.3 7.8 %all-reduce.3 = (f32[336]{0:T(512)S(1)}, f32[32,336]{1,0:T(8,128)S(1)}) all-reduce(f32[336]{0:T(512)} %broadcast_multiply_fusion.3, f32[32,336]{1,0:T(8,128)S(1)} %broadcast_multiply_fusion.2), channel_id=1, replica_groups=mesh['grp'=2,'gen'=4,'row'=2,'ch'=2] {'row'}, use_global_device_ids=true, to_apply=%region_1.2 | all-reduce | flops 11088 | bytes 88704 | tf_op jit(solution)/shard_map/psum | solution.py:77
  96.1 1.9 %all-gather = f32[2,336,32]{1,2,0:T(8,128)S(1)} all-gather(f32[1,336,32]{1,2,0:T(8,128)S(1)} %bitcast.62), channel_id=1, replica_groups=mesh['grp'=2,'gen'=4,'row'=2,'ch'=2] {'ch'}, dimensions={0}, use_global_device_ids=true | all-gather | bytes 129024 | tf_op jit(solution)/shard_map/all_gather | solution.py:80
  98.4 1.0 abs_reduce_fusion.1
  99.4 1.6 %collective-permute-start.4 = (f32[336]{0:T(512)S(1)}, f32[336]{0:T(512)S(1)}, u32[]{:S(2)}, u32[]{:S(2)}) collective-permute-start(f32[336]{0:T(512)S(1)} %get-tuple-element.46), channel_id=1, source_target_pairs={{0,4},{4,0},{8,12},{12,8},{1,5},{5,1},{9,13},{13,9},{2,6},{6,2},{1... | collective-permute-start | bytes 4040 | tf_op jit(solution)/shard_map/ppermute | solution.py:89
  101.2 2.4 %all-reduce.2 = f32[672]{0:T(1024)S(1)} all-reduce(f32[672]{0:T(1024)S(1)} %dynamic-update-slice), channel_id=1, replica_groups=mesh['grp'=2,'gen'=4,'row'=2,'ch'=2] {'ch'}, use_global_device_ids=true, to_apply=%add.2 | all-reduce | flops 672 | bytes 5376
  104.6 2.7 %collective-permute-start.5 = (f32[336]{0:T(512)S(1)}, f32[336]{0:T(512)S(1)}, u32[]{:S(2)}, u32[]{:S(2)}) collective-permute-start(f32[336]{0:T(512)S(1)} %add.263), channel_id=1, source_target_pairs={{0,8},{4,12},{8,0},{12,4},{1,9},{5,13},{9,1},{13,5},{2,10},{6,14},... | collective-permute-start | bytes 4040 | tf_op jit(solution)/shard_map/ppermute | solution.py:89
  109.9 5.0 %fusion.7 = bf16[32,6,24,336]{3,2,1,0:T(8,128)(2,1)} fusion(bf16[32,6,24,336]{3,2,1,0:T(8,128)(2,1)} %copy-done.3, f32[336]{0:T(512)S(1)} %get-tuple-element.44, f32[32,336]{1,0:T(8,128)S(1)} %broadcast_multiply_fusion.1, f32[6,24,336]{2,1,0:T(8,128)} %get-tuple-element.36), kind=kLoop, calls=%fused_computation.11 | loop fusion | flops 7741440 | bytes 6431040 | tf_op jit(solution)/shard_map/convert_element_type | solution.py:98
  114.9 26.4 %all-reduce.6.cloned.1.call-done = bf16[6,24,336]{2,1,0:T(8,128)(2,1)} async-done(((bf16[6,24,336]{2,1,0:T(8,128)(2,1)}), bf16[6,24,336]{2,1,0:T(8,128)(2,1)}) %all-reduce.6.cloned.1.call-update) | async-done | bytes 96784 | tf_op jit(solution)/shard_map/psum | solution.py:73
  141.3 1.7 %multiply_add_fusion = (f32[6,24,336]{2,1,0:T(8,128)}, f32[6,24,336]{2,1,0:T(8,128)}) fusion(bf16[6,24,336]{2,1,0:T(8,128)(2,1)} %all-reduce.6.cloned.1.call-done, f32[6,24,336]{2,1,0:T(8,128)S(1)} %copy-done.5, f32[336]{0:T(512)S(1)} %get-tuple-element.43, f32[336]{0:T(512)S(1)} %get-tuple-element.30, f32[336]{0:T(512)S(1)} %get-tuple-element.44), kind=kLoop, calls=%fused_computation.77 | loop fusion | flops 290304 | bytes 681408 | tf_op jit(solution)/shard_map/add | solution.py:99
  (85 shorter events, 6.4 us)
Async XLA Ops:
  7.2 42.3 %copy-start.29 = (f32[336]{0:T(512)S(1)}, f32[336]{0:T(512)}, u32[]{:S(2)}) copy-start(f32[336]{0:T(512)} %param.15) | copy-start | bytes 4036
  7.2 134.0 %all-reduce.6.cloned.1.call-start = ((), (), s32[]{:S(2)}) async-start(), calls=%async_computation | async-start | bytes 221184 | tf_op jit(solution)/shard_map/psum | solution.py:73
  14.3 37.2 %collective-permute-start.2 = (bf16[32,2,24,336]{3,2,1,0:T(8,128)(2,1)}, bf16[32,2,24,336]{3,2,1,0:T(8,128)(2,1)S(1)}, u32[]{:S(2)}, u32[]{:S(2)}) collective-permute-start(bf16[32,2,24,336]{3,2,1,0:T(8,128)(2,1)} %get-tuple-element.37), channel_id=1, source_target_pairs={{0,2},{1,3},{4,6},{5,7},{8,10},{9,11},{12,14},{13,15},{16,18},{17,... | collective-permute-start | bytes 3096584 | tf_op jit(solution)/shard_map/ppermute | solution.py:15
  19.2 33.5 %collective-permute-start.3 = (bf16[32,2,24,336]{3,2,1,0:T(8,128)(2,1)}, bf16[32,2,24,336]{3,2,1,0:T(8,128)(2,1)}, u32[]{:S(2)}, u32[]{:S(2)}) collective-permute-start(bf16[32,2,24,336]{3,2,1,0:T(8,128)(2,1)} %get-tuple-element.38), channel_id=1, source_target_pairs={{2,0},{3,1},{6,4},{7,5},{10,8},{11,9},{14,12},{15,13},{18,16},{19,... | collective-permute-start | bytes 3096584 | tf_op jit(solution)/shard_map/ppermute | solution.py:17
  20.7 24.6 %collective-permute-start = (bf16[1,2,24,336]{3,2,1,0:T(8,128)(2,1)S(1)}, bf16[1,2,24,336]{3,2,1,0:T(8,128)(2,1)S(1)}, u32[]{:S(2)}, u32[]{:S(2)}) collective-permute-start(bf16[1,2,24,336]{3,2,1,0:T(8,128)(2,1)S(1)} %get-tuple-element.41), channel_id=1, source_target_pairs={{0,2},{1,3},{4,6},{5,7},{8,10},{9,11},{12,14},{13,15},{16,18},{17,... | collective-permute-start | bytes 96776 | tf_op jit(solution)/shard_map/ppermute | solution.py:15
  26.3 23.2 %collective-permute-start.1 = (bf16[1,2,24,336]{3,2,1,0:T(8,128)(2,1)S(1)}, bf16[1,2,24,336]{3,2,1,0:T(8,128)(2,1)S(1)}, u32[]{:S(2)}, u32[]{:S(2)}) collective-permute-start(bf16[1,2,24,336]{3,2,1,0:T(8,128)(2,1)S(1)} %get-tuple-element.42), channel_id=1, source_target_pairs={{2,0},{3,1},{6,4},{7,5},{10,8},{11,9},{14,12},{15,13},{18,16},{19,... | collective-permute-start | bytes 96776 | tf_op jit(solution)/shard_map/ppermute | solution.py:17
  27.7 23.8 %copy-start.10 = (f32[336]{0:T(512)}, f32[336]{0:T(512)S(1)}, u32[]{:S(2)}) copy-start(f32[336]{0:T(512)S(1)} %get-tuple-element.10) | copy-start | bytes 4036
  27.7 23.8 %copy-start.11 = (f32[336]{0:T(512)}, f32[336]{0:T(512)S(1)}, u32[]{:S(2)}) copy-start(f32[336]{0:T(512)S(1)} %get-tuple-element.11) | copy-start | bytes 4036
  27.7 23.8 %copy-start.12 = (f32[336]{0:T(512)}, f32[336]{0:T(512)S(1)}, u32[]{:S(2)}) copy-start(f32[336]{0:T(512)S(1)} %get-tuple-element.12) | copy-start | bytes 4036
  27.7 23.8 %copy-start.13 = (f32[336]{0:T(512)}, f32[336]{0:T(512)S(1)}, u32[]{:S(2)}) copy-start(f32[336]{0:T(512)S(1)} %get-tuple-element.13) | copy-start | bytes 4036
  27.7 23.8 %copy-start.14 = (f32[336]{0:T(512)}, f32[336]{0:T(512)S(1)}, u32[]{:S(2)}) copy-start(f32[336]{0:T(512)S(1)} %get-tuple-element.14) | copy-start | bytes 4036
  27.7 23.8 %copy-start.15 = (f32[336]{0:T(512)}, f32[336]{0:T(512)S(1)}, u32[]{:S(2)}) copy-start(f32[336]{0:T(512)S(1)} %get-tuple-element.15) | copy-start | bytes 4036
  27.8 23.8 %copy-start.16 = (f32[336]{0:T(512)}, f32[336]{0:T(512)S(1)}, u32[]{:S(2)}) copy-start(f32[336]{0:T(512)S(1)} %get-tuple-element.16) | copy-start | bytes 4036
  27.8 23.8 %copy-start.17 = (f32[336]{0:T(512)}, f32[336]{0:T(512)S(1)}, u32[]{:S(2)}) copy-start(f32[336]{0:T(512)S(1)} %get-tuple-element.17) | copy-start | bytes 4036
  27.8 23.8 %copy-start.18 = (f32[336]{0:T(512)}, f32[336]{0:T(512)S(1)}, u32[]{:S(2)}) copy-start(f32[336]{0:T(512)S(1)} %get-tuple-element.18) | copy-start | bytes 4036
  27.8 23.8 %copy-start.19 = (f32[336]{0:T(512)}, f32[336]{0:T(512)S(1)}, u32[]{:S(2)}) copy-start(f32[336]{0:T(512)S(1)} %get-tuple-element.19) | copy-start | bytes 4036
  27.8 23.8 %copy-start.20 = (f32[336]{0:T(512)}, f32[336]{0:T(512)S(1)}, u32[]{:S(2)}) copy-start(f32[336]{0:T(512)S(1)} %get-tuple-element.20) | copy-start | bytes 4036
  27.8 23.8 %copy-start.21 = (f32[336]{0:T(512)}, f32[336]{0:T(512)S(1)}, u32[]{:S(2)}) copy-start(f32[336]{0:T(512)S(1)} %get-tuple-element.21) | copy-start | bytes 4036
  27.9 23.8 %copy-start.23 = (f32[336]{0:T(512)}, f32[336]{0:T(512)S(1)}, u32[]{:S(2)}) copy-start(f32[336]{0:T(512)S(1)} %get-tuple-element.23) | copy-start | bytes 4036
  27.9 23.8 %copy-start.24 = (f32[336]{0:T(512)}, f32[336]{0:T(512)S(1)}, u32[]{:S(2)}) copy-start(f32[336]{0:T(512)S(1)} %get-tuple-element.24) | copy-start | bytes 4036
  58.4 39.7 %copy-start.6 = (f32[672,28]{0,1:T(8,128)S(1)}, f32[672,28]{0,1:T(8,128)}, u32[]{:S(2)}) copy-start(f32[672,28]{0,1:T(8,128)} %param.16) | copy-start | bytes 225796
  85.9 55.4 %copy-start.5 = (f32[6,24,336]{2,1,0:T(8,128)S(1)}, f32[6,24,336]{2,1,0:T(8,128)}, u32[]{:S(2)}) copy-start(f32[6,24,336]{2,1,0:T(8,128)} %get-tuple-element.36) | copy-start | bytes 580612
  99.4 5.1 %collective-permute-start.4 = (f32[336]{0:T(512)S(1)}, f32[336]{0:T(512)S(1)}, u32[]{:S(2)}, u32[]{:S(2)}) collective-permute-start(f32[336]{0:T(512)S(1)} %get-tuple-element.46), channel_id=1, source_target_pairs={{0,4},{4,0},{8,12},{12,8},{1,5},{5,1},{9,13},{13,9},{2,6},{6,2},{1... | collective-permute-start | bytes 4040 | tf_op jit(solution)/shard_map/ppermute | solution.py:89
  104.6 4.5 %collective-permute-start.5 = (f32[336]{0:T(512)S(1)}, f32[336]{0:T(512)S(1)}, u32[]{:S(2)}, u32[]{:S(2)}) collective-permute-start(f32[336]{0:T(512)S(1)} %add.263), channel_id=1, source_target_pairs={{0,8},{4,12},{8,0},{12,4},{1,9},{5,13},{9,1},{13,5},{2,10},{6,14},... | collective-permute-start | bytes 4040 | tf_op jit(solution)/shard_map/ppermute | solution.py:89
  (14 other events, 190.8 us)
Sparse Core Ops, SparseCore 0:
  108.3 32.9 all-reduce.5
